TPU v7x, 512 devices: a whole 4x4x16 slice. The times are simulated.
512 devices in a mesh: sub: 32 (over z_hi, x, core), lev: 16 (over y, z_lo).
Axes of the slice: x: 4, y: 4, z: 16 (z_hi: 4, z_lo: 4; z = z_hi * 4 + z_lo), core: 2. Of those that a mesh axis runs over, the one named last changes fastest.
Arguments:
- increment: float32 [6, 128, 64, 4096], P(None, 'lev', None, 'sub'), may hold values from -6 to 6
- std_dev: float32 [6, 128], P(None, 'lev'), may hold values from 0.5 to 2
- land_mask: int32 [64, 4096], P(None, 'sub'), may hold values 0 or 1
- row_class: int32 [64], replicated, may hold values from 0 to 7
- column_class: int32 [4096], P('sub'), may hold values from 0 to 7
- vertical_modes: float32 [6, 128, 128], replicated, as said below
- mode_variance: float32 [6, 128], replicated, may hold values from 0.25 to 4
Outputs:
- covaried: float32 [6, 128, 64, 4096], P(None, 'lev', None, 'sub')
Inputs may be any that keep to these rules, and one draw needn't show every extreme that they name: `vertical_modes`: each variable's matrix is the identity plus independent entries of deviation 0.5 / sqrt(128).
All inputs are finite; a program needn't handle non-finite values. No bound on the sum of `land_mask` on one device may be relied on, other than what follows from the above.
Results may differ from a plain program's by a relative error of at most 0.0003.
Values sent between devices are 32-bit elements; how exact they have to be, the bound alone decides.
A program may use at most 64 MiB of HBM per device.

v0:
```python
import jax
import jax.numpy as jnp
from jax import lax
from jax.sharding import PartitionSpec as P


def passed_along(array, axis, by):
    size = lax.axis_size(axis)
    pairs = [(i, i + by) for i in range(size) if 0 <= i + by < size]
    return lax.ppermute(array, axis, pairs)


def rate_table(length, fast_one, fast_two):
    return jnp.array(
        [
            fast_one,
            fast_two,
            0.3 / length,
            0.6 / length,
            1.0 / length,
            1.4 / length,
            1.8 / length,
            2.2 / length,
        ],
        jnp.float32,
    )


def decay_lookup(classes, rates):
    matches = classes[:, None] == jnp.arange(8, dtype=jnp.int32)[None, :]
    return jnp.sum(jnp.where(matches, jnp.exp(-rates)[None, :], 0.0), axis=1)


def filter_rows(decays, length):
    position = jnp.arange(length)
    distance = jnp.maximum(position[:, None] - position[None, :], 0).astype(jnp.float32)
    log_decay = jnp.log(decays)
    scaling = jnp.sqrt(1.0 - decays * decays)
    kernel = jnp.exp(distance[None] * log_decay[:, None, None]) * scaling[:, None, None]
    return jnp.where((position[:, None] >= position[None, :])[None], kernel, 0.0)


def carry_in(through, outgoing, backward):
    devices = lax.axis_size("sub")

    def relay_step(counter, received):
        outgoing_now = through * received + outgoing
        if backward:
            return passed_along(outgoing_now, "sub", -1)
        return passed_along(outgoing_now, "sub", 1)

    return lax.fori_loop(0, devices - 1, relay_step, jnp.zeros_like(outgoing))


def sweep_along(grid_field, decays, backward):
    span_x = grid_field.shape[3]
    kernel = filter_rows(decays, span_x)
    log_decay = jnp.log(decays)
    position = jnp.arange(span_x, dtype=jnp.float32)
    through = jnp.exp(span_x * log_decay)
    if backward:
        inside = jnp.einsum("vlyi,yij->vlyj", grid_field, kernel, precision=lax.Precision.HIGHEST)
        outgoing = inside[..., 0]
        decays_in = jnp.exp((span_x - position)[None, :] * log_decay[:, None])
    else:
        inside = jnp.einsum("vlyj,yij->vlyi", grid_field, kernel, precision=lax.Precision.HIGHEST)
        outgoing = inside[..., span_x - 1]
        decays_in = jnp.exp((position + 1.0)[None, :] * log_decay[:, None])
    incoming = carry_in(through, outgoing, backward)
    return inside + incoming[..., None] * decays_in[None, None]


def project_modes(level_slab, vertical_modes, mode_variance):
    amplitude = jnp.einsum(
        "vlm,vlrc->vmrc", vertical_modes, level_slab, precision=lax.Precision.HIGHEST
    )
    amplitude = amplitude * mode_variance[:, :, None, None]
    return jnp.einsum("vlm,vmrc->vlrc", vertical_modes, amplitude, precision=lax.Precision.HIGHEST)


def on_device(
    increment, std_dev, land_mask, row_class, column_class, vertical_modes, mode_variance
):
    row_count = increment.shape[2]
    total_x = increment.shape[3] * lax.axis_size("sub")
    decay_rows = decay_lookup(row_class, rate_table(total_x, 1.0 / 24, 1.0 / 40))
    decay_cols = decay_lookup(column_class, rate_table(row_count, 1.0 / 8, 1.0 / 12))
    kernel_cols = filter_rows(decay_cols, row_count)
    weights = std_dev[:, :, None, None] * (1.0 + 0.8 * land_mask.astype(jnp.float32))[None, None]
    state = weights * increment
    state = sweep_along(state, decay_rows, True)
    state = jnp.einsum("vlix,xij->vljx", state, kernel_cols, precision=lax.Precision.HIGHEST)
    mixed = project_modes(
        lax.all_to_all(state, "lev", split_axis=2, concat_axis=1, tiled=True),
        vertical_modes,
        mode_variance,
    )
    state = lax.all_to_all(mixed, "lev", split_axis=1, concat_axis=2, tiled=True)
    state = jnp.einsum("vljx,xij->vlix", state, kernel_cols, precision=lax.Precision.HIGHEST)
    state = sweep_along(state, decay_rows, False)
    return weights * state


def solution(mesh):
    return jax.shard_map(
        on_device,
        mesh=mesh,
        in_specs=(
            P(None, "lev", None, "sub"),
            P(None, "lev"),
            P(None, "sub"),
            P(),
            P("sub"),
            P(),
            P(),
        ),
        out_specs=P(None, "lev", None, "sub"),
        check_vma=False,
    )
```

profile of v0, /device:TPU:384, one launch (start us, length us, event | category | flops | bytes accessed | tf_op | source)
XLA Modules:
  0.0 850.2 jit_solution(4033541890119137354)
XLA Ops:
  9.4 343.5 %while.20 = (s32[]{:T(128)}, f32[6,8,64]{2,1,0:T(8,128)S(1)}, f32[64]{0:T(128)S(1)}, f32[6,8,64]{2,1,0:T(8,128)S(1)}, s32[]{:T(128)}) while((s32[]{:T(128)}, f32[6,8,64]{2,1,0:T(8,128)S(1)}, f32[64]{0:T(128)S(1)}, f32[6,8,64]{2,1,0:T(8,128)S(1)}, s32[]{:T(128)}) %tuple.44), condition=%wide.region_3.4_spmd, body=%wide.region_2.3_spmd.sunk | while | flops 6146 | bytes 86373 | solution.py:52
  18.2 9.6 %collective-permute-start = (f32[6,8,64]{2,1,0:T(8,128)S(1)}, f32[6,8,64]{2,1,0:T(8,128)S(1)}, u32[]{:S(2)}, u32[]{:S(2)}) collective-permute-start(f32[6,8,64]{2,1,0:T(8,128)S(1)} %multiply_add_fusion.6), channel_id=1, source_target_pairs={{16,0},{32,16},{48,32},{64,48},{80,64},{96,80},{112,96},{128,112},... | collective-permute-start | bytes 36872 | tf_op jit(solution)/shard_map/while/body/eval_jaxpr/ppermute | solution.py:10
  29.4 9.6 %collective-permute-start = (f32[6,8,64]{2,1,0:T(8,128)S(1)}, f32[6,8,64]{2,1,0:T(8,128)S(1)}, u32[]{:S(2)}, u32[]{:S(2)}) collective-permute-start(f32[6,8,64]{2,1,0:T(8,128)S(1)} %multiply_add_fusion.6), channel_id=1, source_target_pairs={{16,0},{32,16},{48,32},{64,48},{80,64},{96,80},{112,96},{128,112},... | collective-permute-start | bytes 36872 | tf_op jit(solution)/shard_map/while/body/eval_jaxpr/ppermute | solution.py:10
  40.5 9.6 %collective-permute-start = (f32[6,8,64]{2,1,0:T(8,128)S(1)}, f32[6,8,64]{2,1,0:T(8,128)S(1)}, u32[]{:S(2)}, u32[]{:S(2)}) collective-permute-start(f32[6,8,64]{2,1,0:T(8,128)S(1)} %multiply_add_fusion.6), channel_id=1, source_target_pairs={{16,0},{32,16},{48,32},{64,48},{80,64},{96,80},{112,96},{128,112},... | collective-permute-start | bytes 36872 | tf_op jit(solution)/shard_map/while/body/eval_jaxpr/ppermute | solution.py:10
  51.7 9.6 %collective-permute-start = (f32[6,8,64]{2,1,0:T(8,128)S(1)}, f32[6,8,64]{2,1,0:T(8,128)S(1)}, u32[]{:S(2)}, u32[]{:S(2)}) collective-permute-start(f32[6,8,64]{2,1,0:T(8,128)S(1)} %multiply_add_fusion.6), channel_id=1, source_target_pairs={{16,0},{32,16},{48,32},{64,48},{80,64},{96,80},{112,96},{128,112},... | collective-permute-start | bytes 36872 | tf_op jit(solution)/shard_map/while/body/eval_jaxpr/ppermute | solution.py:10
  62.9 9.6 %collective-permute-start = (f32[6,8,64]{2,1,0:T(8,128)S(1)}, f32[6,8,64]{2,1,0:T(8,128)S(1)}, u32[]{:S(2)}, u32[]{:S(2)}) collective-permute-start(f32[6,8,64]{2,1,0:T(8,128)S(1)} %multiply_add_fusion.6), channel_id=1, source_target_pairs={{16,0},{32,16},{48,32},{64,48},{80,64},{96,80},{112,96},{128,112},... | collective-permute-start | bytes 36872 | tf_op jit(solution)/shard_map/while/body/eval_jaxpr/ppermute | solution.py:10
  74.0 9.6 %collective-permute-start = (f32[6,8,64]{2,1,0:T(8,128)S(1)}, f32[6,8,64]{2,1,0:T(8,128)S(1)}, u32[]{:S(2)}, u32[]{:S(2)}) collective-permute-start(f32[6,8,64]{2,1,0:T(8,128)S(1)} %multiply_add_fusion.6), channel_id=1, source_target_pairs={{16,0},{32,16},{48,32},{64,48},{80,64},{96,80},{112,96},{128,112},... | collective-permute-start | bytes 36872 | tf_op jit(solution)/shard_map/while/body/eval_jaxpr/ppermute | solution.py:10
  85.2 9.6 %collective-permute-start = (f32[6,8,64]{2,1,0:T(8,128)S(1)}, f32[6,8,64]{2,1,0:T(8,128)S(1)}, u32[]{:S(2)}, u32[]{:S(2)}) collective-permute-start(f32[6,8,64]{2,1,0:T(8,128)S(1)} %multiply_add_fusion.6), channel_id=1, source_target_pairs={{16,0},{32,16},{48,32},{64,48},{80,64},{96,80},{112,96},{128,112},... | collective-permute-start | bytes 36872 | tf_op jit(solution)/shard_map/while/body/eval_jaxpr/ppermute | solution.py:10
  96.3 9.6 %collective-permute-start = (f32[6,8,64]{2,1,0:T(8,128)S(1)}, f32[6,8,64]{2,1,0:T(8,128)S(1)}, u32[]{:S(2)}, u32[]{:S(2)}) collective-permute-start(f32[6,8,64]{2,1,0:T(8,128)S(1)} %multiply_add_fusion.6), channel_id=1, source_target_pairs={{16,0},{32,16},{48,32},{64,48},{80,64},{96,80},{112,96},{128,112},... | collective-permute-start | bytes 36872 | tf_op jit(solution)/shard_map/while/body/eval_jaxpr/ppermute | solution.py:10
  107.5 9.6 %collective-permute-start = (f32[6,8,64]{2,1,0:T(8,128)S(1)}, f32[6,8,64]{2,1,0:T(8,128)S(1)}, u32[]{:S(2)}, u32[]{:S(2)}) collective-permute-start(f32[6,8,64]{2,1,0:T(8,128)S(1)} %multiply_add_fusion.6), channel_id=1, source_target_pairs={{16,0},{32,16},{48,32},{64,48},{80,64},{96,80},{112,96},{128,112},... | collective-permute-start | bytes 36872 | tf_op jit(solution)/shard_map/while/body/eval_jaxpr/ppermute | solution.py:10
  152.1 9.6 %collective-permute-start = (f32[6,8,64]{2,1,0:T(8,128)S(1)}, f32[6,8,64]{2,1,0:T(8,128)S(1)}, u32[]{:S(2)}, u32[]{:S(2)}) collective-permute-start(f32[6,8,64]{2,1,0:T(8,128)S(1)} %multiply_add_fusion.6), channel_id=1, source_target_pairs={{16,0},{32,16},{48,32},{64,48},{80,64},{96,80},{112,96},{128,112},... | collective-permute-start | bytes 36872 | tf_op jit(solution)/shard_map/while/body/eval_jaxpr/ppermute | solution.py:10
  163.3 9.6 %collective-permute-start = (f32[6,8,64]{2,1,0:T(8,128)S(1)}, f32[6,8,64]{2,1,0:T(8,128)S(1)}, u32[]{:S(2)}, u32[]{:S(2)}) collective-permute-start(f32[6,8,64]{2,1,0:T(8,128)S(1)} %multiply_add_fusion.6), channel_id=1, source_target_pairs={{16,0},{32,16},{48,32},{64,48},{80,64},{96,80},{112,96},{128,112},... | collective-permute-start | bytes 36872 | tf_op jit(solution)/shard_map/while/body/eval_jaxpr/ppermute | solution.py:10
  174.4 9.6 %collective-permute-start = (f32[6,8,64]{2,1,0:T(8,128)S(1)}, f32[6,8,64]{2,1,0:T(8,128)S(1)}, u32[]{:S(2)}, u32[]{:S(2)}) collective-permute-start(f32[6,8,64]{2,1,0:T(8,128)S(1)} %multiply_add_fusion.6), channel_id=1, source_target_pairs={{16,0},{32,16},{48,32},{64,48},{80,64},{96,80},{112,96},{128,112},... | collective-permute-start | bytes 36872 | tf_op jit(solution)/shard_map/while/body/eval_jaxpr/ppermute | solution.py:10
  185.6 9.6 %collective-permute-start = (f32[6,8,64]{2,1,0:T(8,128)S(1)}, f32[6,8,64]{2,1,0:T(8,128)S(1)}, u32[]{:S(2)}, u32[]{:S(2)}) collective-permute-start(f32[6,8,64]{2,1,0:T(8,128)S(1)} %multiply_add_fusion.6), channel_id=1, source_target_pairs={{16,0},{32,16},{48,32},{64,48},{80,64},{96,80},{112,96},{128,112},... | collective-permute-start | bytes 36872 | tf_op jit(solution)/shard_map/while/body/eval_jaxpr/ppermute | solution.py:10
  196.8 9.6 %collective-permute-start = (f32[6,8,64]{2,1,0:T(8,128)S(1)}, f32[6,8,64]{2,1,0:T(8,128)S(1)}, u32[]{:S(2)}, u32[]{:S(2)}) collective-permute-start(f32[6,8,64]{2,1,0:T(8,128)S(1)} %multiply_add_fusion.6), channel_id=1, source_target_pairs={{16,0},{32,16},{48,32},{64,48},{80,64},{96,80},{112,96},{128,112},... | collective-permute-start | bytes 36872 | tf_op jit(solution)/shard_map/while/body/eval_jaxpr/ppermute | solution.py:10
  207.9 9.6 %collective-permute-start = (f32[6,8,64]{2,1,0:T(8,128)S(1)}, f32[6,8,64]{2,1,0:T(8,128)S(1)}, u32[]{:S(2)}, u32[]{:S(2)}) collective-permute-start(f32[6,8,64]{2,1,0:T(8,128)S(1)} %multiply_add_fusion.6), channel_id=1, source_target_pairs={{16,0},{32,16},{48,32},{64,48},{80,64},{96,80},{112,96},{128,112},... | collective-permute-start | bytes 36872 | tf_op jit(solution)/shard_map/while/body/eval_jaxpr/ppermute | solution.py:10
  219.1 9.6 %collective-permute-start = (f32[6,8,64]{2,1,0:T(8,128)S(1)}, f32[6,8,64]{2,1,0:T(8,128)S(1)}, u32[]{:S(2)}, u32[]{:S(2)}) collective-permute-start(f32[6,8,64]{2,1,0:T(8,128)S(1)} %multiply_add_fusion.6), channel_id=1, source_target_pairs={{16,0},{32,16},{48,32},{64,48},{80,64},{96,80},{112,96},{128,112},... | collective-permute-start | bytes 36872 | tf_op jit(solution)/shard_map/while/body/eval_jaxpr/ppermute | solution.py:10
  230.2 9.6 %collective-permute-start = (f32[6,8,64]{2,1,0:T(8,128)S(1)}, f32[6,8,64]{2,1,0:T(8,128)S(1)}, u32[]{:S(2)}, u32[]{:S(2)}) collective-permute-start(f32[6,8,64]{2,1,0:T(8,128)S(1)} %multiply_add_fusion.6), channel_id=1, source_target_pairs={{16,0},{32,16},{48,32},{64,48},{80,64},{96,80},{112,96},{128,112},... | collective-permute-start | bytes 36872 | tf_op jit(solution)/shard_map/while/body/eval_jaxpr/ppermute | solution.py:10
  241.4 9.6 %collective-permute-start = (f32[6,8,64]{2,1,0:T(8,128)S(1)}, f32[6,8,64]{2,1,0:T(8,128)S(1)}, u32[]{:S(2)}, u32[]{:S(2)}) collective-permute-start(f32[6,8,64]{2,1,0:T(8,128)S(1)} %multiply_add_fusion.6), channel_id=1, source_target_pairs={{16,0},{32,16},{48,32},{64,48},{80,64},{96,80},{112,96},{128,112},... | collective-permute-start | bytes 36872 | tf_op jit(solution)/shard_map/while/body/eval_jaxpr/ppermute | solution.py:10
  368.7 37.0 %all_to_all.36 = f32[6,8,64,128]{3,1,0,2:T(8,128)S(1)} all-to-all(f32[6,8,64,128]{3,1,0,2:T(8,128)S(1)} %copy.48), channel_id=1, replica_groups=mesh['sub'=32,'lev'=16] {'lev'}, dimensions={2} | all-to-all | bytes 3145728 | tf_op jit(solution)/shard_map/all_to_all | solution.py:94
  410.7 39.5 %all_to_all.37 = f32[6,128,4,128]{3,2,0,1:T(4,128)S(1)} all-to-all(f32[6,128,4,128]{3,2,0,1:T(4,128)S(1)} %copy.52), channel_id=1, replica_groups=mesh['sub'=32,'lev'=16] {'lev'}, dimensions={1} | all-to-all | bytes 3145728 | tf_op jit(solution)/shard_map/all_to_all | solution.py:98
  454.2 9.9 %fusion.29 = f32[6,8,64,128]{2,1,0,3:T(8,128)} fusion(f32[6,8,64,128]{2,1,0,3:T(8,128)S(1)} %copy.55, f32[128]{0:T(128)} %copy-done.7, f32[128]{0:T(128)} %copy-done.6, f32[64,64]{1,0:T(8,128)} %maximum_convert_fusion.1, pred[64,64]{1,0:T(8,128)(4,1)S(1)} %iota_compare_fusion.1), kind=kOutput, calls=%fused_computation.33 | convolution fusion | flops 303562752 | bytes 3167232 | tf_op jit(solution)/shard_map/vljx,xij->vlix/dot_general | solution.py:99
  476.5 370.6 %while.21 = (s32[]{:T(128)}, f32[6,8,64]{2,1,0:T(8,128)S(1)}, f32[64]{0:T(128)S(1)}, f32[6,8,64]{2,1,0:T(8,128)}, s32[]{:T(128)}) while((s32[]{:T(128)}, f32[6,8,64]{2,1,0:T(8,128)S(1)}, f32[64]{0:T(128)S(1)}, f32[6,8,64]{2,1,0:T(8,128)}, s32[]{:T(128)}) %tuple.46), condition=%wide.region_5.6_spmd, body=%wide.region_4.5_spmd.sunk | while | flops 6146 | bytes 86373 | solution.py:52
  479.2 11.1 %collective-permute-done.1 = f32[6,8,64]{2,1,0:T(8,128)S(1)} collective-permute-done((f32[6,8,64]{2,1,0:T(8,128)S(1)}, f32[6,8,64]{2,1,0:T(8,128)S(1)}, u32[]{:S(2)}, u32[]{:S(2)}) %collective-permute-start.1) | collective-permute-done | bytes 12320 | tf_op jit(solution)/shard_map/while/body/eval_jaxpr/ppermute | solution.py:10
  (220 shorter events, 578.0 us)
Async XLA Ops:
  18.2 11.2 %collective-permute-start = (f32[6,8,64]{2,1,0:T(8,128)S(1)}, f32[6,8,64]{2,1,0:T(8,128)S(1)}, u32[]{:S(2)}, u32[]{:S(2)}) collective-permute-start(f32[6,8,64]{2,1,0:T(8,128)S(1)} %multiply_add_fusion.6), channel_id=1, source_target_pairs={{16,0},{32,16},{48,32},{64,48},{80,64},{96,80},{112,96},{128,112},... | collective-permute-start | bytes 36872 | tf_op jit(solution)/shard_map/while/body/eval_jaxpr/ppermute | solution.py:10
  29.4 11.2 %collective-permute-start = (f32[6,8,64]{2,1,0:T(8,128)S(1)}, f32[6,8,64]{2,1,0:T(8,128)S(1)}, u32[]{:S(2)}, u32[]{:S(2)}) collective-permute-start(f32[6,8,64]{2,1,0:T(8,128)S(1)} %multiply_add_fusion.6), channel_id=1, source_target_pairs={{16,0},{32,16},{48,32},{64,48},{80,64},{96,80},{112,96},{128,112},... | collective-permute-start | bytes 36872 | tf_op jit(solution)/shard_map/while/body/eval_jaxpr/ppermute | solution.py:10
  40.5 11.2 %collective-permute-start = (f32[6,8,64]{2,1,0:T(8,128)S(1)}, f32[6,8,64]{2,1,0:T(8,128)S(1)}, u32[]{:S(2)}, u32[]{:S(2)}) collective-permute-start(f32[6,8,64]{2,1,0:T(8,128)S(1)} %multiply_add_fusion.6), channel_id=1, source_target_pairs={{16,0},{32,16},{48,32},{64,48},{80,64},{96,80},{112,96},{128,112},... | collective-permute-start | bytes 36872 | tf_op jit(solution)/shard_map/while/body/eval_jaxpr/ppermute | solution.py:10
  51.7 11.2 %collective-permute-start = (f32[6,8,64]{2,1,0:T(8,128)S(1)}, f32[6,8,64]{2,1,0:T(8,128)S(1)}, u32[]{:S(2)}, u32[]{:S(2)}) collective-permute-start(f32[6,8,64]{2,1,0:T(8,128)S(1)} %multiply_add_fusion.6), channel_id=1, source_target_pairs={{16,0},{32,16},{48,32},{64,48},{80,64},{96,80},{112,96},{128,112},... | collective-permute-start | bytes 36872 | tf_op jit(solution)/shard_map/while/body/eval_jaxpr/ppermute | solution.py:10
  62.9 11.2 %collective-permute-start = (f32[6,8,64]{2,1,0:T(8,128)S(1)}, f32[6,8,64]{2,1,0:T(8,128)S(1)}, u32[]{:S(2)}, u32[]{:S(2)}) collective-permute-start(f32[6,8,64]{2,1,0:T(8,128)S(1)} %multiply_add_fusion.6), channel_id=1, source_target_pairs={{16,0},{32,16},{48,32},{64,48},{80,64},{96,80},{112,96},{128,112},... | collective-permute-start | bytes 36872 | tf_op jit(solution)/shard_map/while/body/eval_jaxpr/ppermute | solution.py:10
  74.0 11.2 %collective-permute-start = (f32[6,8,64]{2,1,0:T(8,128)S(1)}, f32[6,8,64]{2,1,0:T(8,128)S(1)}, u32[]{:S(2)}, u32[]{:S(2)}) collective-permute-start(f32[6,8,64]{2,1,0:T(8,128)S(1)} %multiply_add_fusion.6), channel_id=1, source_target_pairs={{16,0},{32,16},{48,32},{64,48},{80,64},{96,80},{112,96},{128,112},... | collective-permute-start | bytes 36872 | tf_op jit(solution)/shard_map/while/body/eval_jaxpr/ppermute | solution.py:10
  85.2 11.2 %collective-permute-start = (f32[6,8,64]{2,1,0:T(8,128)S(1)}, f32[6,8,64]{2,1,0:T(8,128)S(1)}, u32[]{:S(2)}, u32[]{:S(2)}) collective-permute-start(f32[6,8,64]{2,1,0:T(8,128)S(1)} %multiply_add_fusion.6), channel_id=1, source_target_pairs={{16,0},{32,16},{48,32},{64,48},{80,64},{96,80},{112,96},{128,112},... | collective-permute-start | bytes 36872 | tf_op jit(solution)/shard_map/while/body/eval_jaxpr/ppermute | solution.py:10
  96.3 11.2 %collective-permute-start = (f32[6,8,64]{2,1,0:T(8,128)S(1)}, f32[6,8,64]{2,1,0:T(8,128)S(1)}, u32[]{:S(2)}, u32[]{:S(2)}) collective-permute-start(f32[6,8,64]{2,1,0:T(8,128)S(1)} %multiply_add_fusion.6), channel_id=1, source_target_pairs={{16,0},{32,16},{48,32},{64,48},{80,64},{96,80},{112,96},{128,112},... | collective-permute-start | bytes 36872 | tf_op jit(solution)/shard_map/while/body/eval_jaxpr/ppermute | solution.py:10
  107.5 11.2 %collective-permute-start = (f32[6,8,64]{2,1,0:T(8,128)S(1)}, f32[6,8,64]{2,1,0:T(8,128)S(1)}, u32[]{:S(2)}, u32[]{:S(2)}) collective-permute-start(f32[6,8,64]{2,1,0:T(8,128)S(1)} %multiply_add_fusion.6), channel_id=1, source_target_pairs={{16,0},{32,16},{48,32},{64,48},{80,64},{96,80},{112,96},{128,112},... | collective-permute-start | bytes 36872 | tf_op jit(solution)/shard_map/while/body/eval_jaxpr/ppermute | solution.py:10
  118.6 11.2 %collective-permute-start = (f32[6,8,64]{2,1,0:T(8,128)S(1)}, f32[6,8,64]{2,1,0:T(8,128)S(1)}, u32[]{:S(2)}, u32[]{:S(2)}) collective-permute-start(f32[6,8,64]{2,1,0:T(8,128)S(1)} %multiply_add_fusion.6), channel_id=1, source_target_pairs={{16,0},{32,16},{48,32},{64,48},{80,64},{96,80},{112,96},{128,112},... | collective-permute-start | bytes 36872 | tf_op jit(solution)/shard_map/while/body/eval_jaxpr/ppermute | solution.py:10
  129.8 11.2 %collective-permute-start = (f32[6,8,64]{2,1,0:T(8,128)S(1)}, f32[6,8,64]{2,1,0:T(8,128)S(1)}, u32[]{:S(2)}, u32[]{:S(2)}) collective-permute-start(f32[6,8,64]{2,1,0:T(8,128)S(1)} %multiply_add_fusion.6), channel_id=1, source_target_pairs={{16,0},{32,16},{48,32},{64,48},{80,64},{96,80},{112,96},{128,112},... | collective-permute-start | bytes 36872 | tf_op jit(solution)/shard_map/while/body/eval_jaxpr/ppermute | solution.py:10
  196.8 11.2 %collective-permute-start = (f32[6,8,64]{2,1,0:T(8,128)S(1)}, f32[6,8,64]{2,1,0:T(8,128)S(1)}, u32[]{:S(2)}, u32[]{:S(2)}) collective-permute-start(f32[6,8,64]{2,1,0:T(8,128)S(1)} %multiply_add_fusion.6), channel_id=1, source_target_pairs={{16,0},{32,16},{48,32},{64,48},{80,64},{96,80},{112,96},{128,112},... | collective-permute-start | bytes 36872 | tf_op jit(solution)/shard_map/while/body/eval_jaxpr/ppermute | solution.py:10
  207.9 11.2 %collective-permute-start = (f32[6,8,64]{2,1,0:T(8,128)S(1)}, f32[6,8,64]{2,1,0:T(8,128)S(1)}, u32[]{:S(2)}, u32[]{:S(2)}) collective-permute-start(f32[6,8,64]{2,1,0:T(8,128)S(1)} %multiply_add_fusion.6), channel_id=1, source_target_pairs={{16,0},{32,16},{48,32},{64,48},{80,64},{96,80},{112,96},{128,112},... | collective-permute-start | bytes 36872 | tf_op jit(solution)/shard_map/while/body/eval_jaxpr/ppermute | solution.py:10
  219.1 11.2 %collective-permute-start = (f32[6,8,64]{2,1,0:T(8,128)S(1)}, f32[6,8,64]{2,1,0:T(8,128)S(1)}, u32[]{:S(2)}, u32[]{:S(2)}) collective-permute-start(f32[6,8,64]{2,1,0:T(8,128)S(1)} %multiply_add_fusion.6), channel_id=1, source_target_pairs={{16,0},{32,16},{48,32},{64,48},{80,64},{96,80},{112,96},{128,112},... | collective-permute-start | bytes 36872 | tf_op jit(solution)/shard_map/while/body/eval_jaxpr/ppermute | solution.py:10
  230.2 11.2 %collective-permute-start = (f32[6,8,64]{2,1,0:T(8,128)S(1)}, f32[6,8,64]{2,1,0:T(8,128)S(1)}, u32[]{:S(2)}, u32[]{:S(2)}) collective-permute-start(f32[6,8,64]{2,1,0:T(8,128)S(1)} %multiply_add_fusion.6), channel_id=1, source_target_pairs={{16,0},{32,16},{48,32},{64,48},{80,64},{96,80},{112,96},{128,112},... | collective-permute-start | bytes 36872 | tf_op jit(solution)/shard_map/while/body/eval_jaxpr/ppermute | solution.py:10
  241.4 11.2 %collective-permute-start = (f32[6,8,64]{2,1,0:T(8,128)S(1)}, f32[6,8,64]{2,1,0:T(8,128)S(1)}, u32[]{:S(2)}, u32[]{:S(2)}) collective-permute-start(f32[6,8,64]{2,1,0:T(8,128)S(1)} %multiply_add_fusion.6), channel_id=1, source_target_pairs={{16,0},{32,16},{48,32},{64,48},{80,64},{96,80},{112,96},{128,112},... | collective-permute-start | bytes 36872 | tf_op jit(solution)/shard_map/while/body/eval_jaxpr/ppermute | solution.py:10
  252.5 11.2 %collective-permute-start = (f32[6,8,64]{2,1,0:T(8,128)S(1)}, f32[6,8,64]{2,1,0:T(8,128)S(1)}, u32[]{:S(2)}, u32[]{:S(2)}) collective-permute-start(f32[6,8,64]{2,1,0:T(8,128)S(1)} %multiply_add_fusion.6), channel_id=1, source_target_pairs={{16,0},{32,16},{48,32},{64,48},{80,64},{96,80},{112,96},{128,112},... | collective-permute-start | bytes 36872 | tf_op jit(solution)/shard_map/while/body/eval_jaxpr/ppermute | solution.py:10
  263.7 11.2 %collective-permute-start = (f32[6,8,64]{2,1,0:T(8,128)S(1)}, f32[6,8,64]{2,1,0:T(8,128)S(1)}, u32[]{:S(2)}, u32[]{:S(2)}) collective-permute-start(f32[6,8,64]{2,1,0:T(8,128)S(1)} %multiply_add_fusion.6), channel_id=1, source_target_pairs={{16,0},{32,16},{48,32},{64,48},{80,64},{96,80},{112,96},{128,112},... | collective-permute-start | bytes 36872 | tf_op jit(solution)/shard_map/while/body/eval_jaxpr/ppermute | solution.py:10
  274.9 11.2 %collective-permute-start = (f32[6,8,64]{2,1,0:T(8,128)S(1)}, f32[6,8,64]{2,1,0:T(8,128)S(1)}, u32[]{:S(2)}, u32[]{:S(2)}) collective-permute-start(f32[6,8,64]{2,1,0:T(8,128)S(1)} %multiply_add_fusion.6), channel_id=1, source_target_pairs={{16,0},{32,16},{48,32},{64,48},{80,64},{96,80},{112,96},{128,112},... | collective-permute-start | bytes 36872 | tf_op jit(solution)/shard_map/while/body/eval_jaxpr/ppermute | solution.py:10
  286.0 11.2 %collective-permute-start = (f32[6,8,64]{2,1,0:T(8,128)S(1)}, f32[6,8,64]{2,1,0:T(8,128)S(1)}, u32[]{:S(2)}, u32[]{:S(2)}) collective-permute-start(f32[6,8,64]{2,1,0:T(8,128)S(1)} %multiply_add_fusion.6), channel_id=1, source_target_pairs={{16,0},{32,16},{48,32},{64,48},{80,64},{96,80},{112,96},{128,112},... | collective-permute-start | bytes 36872 | tf_op jit(solution)/shard_map/while/body/eval_jaxpr/ppermute | solution.py:10
  297.2 11.2 %collective-permute-start = (f32[6,8,64]{2,1,0:T(8,128)S(1)}, f32[6,8,64]{2,1,0:T(8,128)S(1)}, u32[]{:S(2)}, u32[]{:S(2)}) collective-permute-start(f32[6,8,64]{2,1,0:T(8,128)S(1)} %multiply_add_fusion.6), channel_id=1, source_target_pairs={{16,0},{32,16},{48,32},{64,48},{80,64},{96,80},{112,96},{128,112},... | collective-permute-start | bytes 36872 | tf_op jit(solution)/shard_map/while/body/eval_jaxpr/ppermute | solution.py:10
  308.3 11.2 %collective-permute-start = (f32[6,8,64]{2,1,0:T(8,128)S(1)}, f32[6,8,64]{2,1,0:T(8,128)S(1)}, u32[]{:S(2)}, u32[]{:S(2)}) collective-permute-start(f32[6,8,64]{2,1,0:T(8,128)S(1)} %multiply_add_fusion.6), channel_id=1, source_target_pairs={{16,0},{32,16},{48,32},{64,48},{80,64},{96,80},{112,96},{128,112},... | collective-permute-start | bytes 36872 | tf_op jit(solution)/shard_map/while/body/eval_jaxpr/ppermute | solution.py:10
  319.5 11.2 %collective-permute-start = (f32[6,8,64]{2,1,0:T(8,128)S(1)}, f32[6,8,64]{2,1,0:T(8,128)S(1)}, u32[]{:S(2)}, u32[]{:S(2)}) collective-permute-start(f32[6,8,64]{2,1,0:T(8,128)S(1)} %multiply_add_fusion.6), channel_id=1, source_target_pairs={{16,0},{32,16},{48,32},{64,48},{80,64},{96,80},{112,96},{128,112},... | collective-permute-start | bytes 36872 | tf_op jit(solution)/shard_map/while/body/eval_jaxpr/ppermute | solution.py:10
  477.3 13.0 %collective-permute-start.1 = (f32[6,8,64]{2,1,0:T(8,128)S(1)}, f32[6,8,64]{2,1,0:T(8,128)S(1)}, u32[]{:S(2)}, u32[]{:S(2)}) collective-permute-start(f32[6,8,64]{2,1,0:T(8,128)S(1)} %multiply_add_fusion.7), channel_id=1, source_target_pairs={{0,16},{16,32},{32,48},{48,64},{64,80},{80,96},{96,112},{112,128},... | collective-permute-start | bytes 36872 | tf_op jit(solution)/shard_map/while/body/eval_jaxpr/ppermute | solution.py:10
  (48 other events, 1236.5 us)
where the time goes:
time: 854 us; the launch traced here: 850 us
  starting transfers between devices  356 us (42%)
  waiting for transfers between devices  334 us (39%)
  blocking collectives  76.5 us (9%)
  matrix products  35.6 us (4%)
  other arithmetic  29.8 us (3%)
  local copies, waits for them, and re-layouts  17.1 us (2%)
    ppermute x62, starting transfers between devices, passed_along(): return lax.ppermute(array, axis, pairs)  356 us
    ppermute x62, waiting for transfers between devices, passed_along(): return lax.ppermute(array, axis, pairs)  334 us
    all_to_all x1, blocking collectives, on_device(): lax.all_to_all(mixed, 'lev', split_axis=1, concat_axis=2, tiled=True)  39.5 us
    all_to_all x1, blocking collectives, on_device(): lax.all_to_all(state, 'lev', split_axis=2, concat_axis=1, tiled=True)  37 us
    add x62, other arithmetic, relay_step(): outgoing_now = through * received + outgoing  23.2 us
  transfers between devices with their start and end apart: 62, of which 62 were waited for; matrix products, arithmetic and copies ran while one was open for 0% of the time, Pallas kernels for 0%

commit v1 on v0

--- a/solution.py
+++ b/solution.py
@@ -2,12 +2,6 @@
 import jax.numpy as jnp
 from jax import lax
 from jax.sharding import PartitionSpec as P
-
-
-def passed_along(array, axis, by):
-    size = lax.axis_size(axis)
-    pairs = [(i, i + by) for i in range(size) if 0 <= i + by < size]
-    return lax.ppermute(array, axis, pairs)
 
 
 def rate_table(length, fast_one, fast_two):
@@ -40,16 +34,17 @@
     return jnp.where((position[:, None] >= position[None, :])[None], kernel, 0.0)
 
 
-def carry_in(through, outgoing, backward):
+def carry_in(log_decay, span, outgoing, backward):
     devices = lax.axis_size("sub")
-
-    def relay_step(counter, received):
-        outgoing_now = through * received + outgoing
-        if backward:
-            return passed_along(outgoing_now, "sub", -1)
-        return passed_along(outgoing_now, "sub", 1)
-
-    return lax.fori_loop(0, devices - 1, relay_step, jnp.zeros_like(outgoing))
+    me = lax.axis_index("sub")
+    gathered = lax.all_gather(outgoing, "sub")
+    others = jnp.arange(devices)
+    gap = (others - me if backward else me - others) - 1
+    reach = jnp.maximum(gap, 0).astype(jnp.float32) * span
+    factors = jnp.where(
+        (gap >= 0)[:, None], jnp.exp(reach[:, None] * log_decay[None, :]), 0.0
+    )
+    return jnp.sum(gathered * factors[:, None, None, :], axis=0)
 
 
 def sweep_along(grid_field, decays, backward):
@@ -57,7 +52,6 @@
     kernel = filter_rows(decays, span_x)
     log_decay = jnp.log(decays)
     position = jnp.arange(span_x, dtype=jnp.float32)
-    through = jnp.exp(span_x * log_decay)
     if backward:
         inside = jnp.einsum("vlyi,yij->vlyj", grid_field, kernel, precision=lax.Precision.HIGHEST)
         outgoing = inside[..., 0]
@@ -66,7 +60,7 @@
         inside = jnp.einsum("vlyj,yij->vlyi", grid_field, kernel, precision=lax.Precision.HIGHEST)
         outgoing = inside[..., span_x - 1]
         decays_in = jnp.exp((position + 1.0)[None, :] * log_decay[:, None])
-    incoming = carry_in(through, outgoing, backward)
+    incoming = carry_in(log_decay, span_x, outgoing, backward)
     return inside + incoming[..., None] * decays_in[None, None]
 
 

time: 854 us -> 2520 us (2.95)
  the two profiles are of different devices: /device:TPU:384 before, /device:TPU:75 now
where the time goes in v1:
time: 2520 us
  blocking collectives  2410 us (96%)
  local copies, waits for them, and re-layouts  67.9 us (3%)
  matrix products  34 us (1%)
    all_gather x2, blocking collectives, carry_in(): gathered = lax.all_gather(outgoing, 'sub')  2200 us
    all_to_all x1, blocking collectives, on_device(): lax.all_to_all(state, 'lev', split_axis=2, concat_axis=1, tiled=True)  162 us
    all_gather x2, local copies, waits for them, and re-layouts, carry_in(): gathered = lax.all_gather(outgoing, 'sub')  53 us

profile of v1, /device:TPU:75, one launch (start us, length us, event | category | flops | bytes accessed | tf_op | source)
XLA Modules:
  0.0 2517.8 jit_solution(8854969870332106968)
XLA Ops:
  0.7 0.8 select_reduce_fusion
  2.1 0.8 select_reduce_fusion.1
  2.8 0.8 multiply_add_fusion.1
  3.6 6.5 fusion.48
  10.1 978.8 %all-gather = f32[192,8,64,1]{3,1,0,2:T(8,128)} all-gather(f32[6,8,64,1]{3,1,0,2:T(8,128)S(1)} %bitcast.68), channel_id=2, replica_groups=mesh['sub'=32,'lev'=16] {'sub'}, dimensions={0}, use_global_device_ids=true | all-gather | bytes 405504 | tf_op jit(solution)/shard_map/all_gather | solution.py:40
  988.9 26.5 %copy.39 = f32[192,8,64,1]{2,1,0,3:T(8,128)S(1)} copy(f32[192,8,64,1]{3,1,0,2:T(8,128)} %all-gather) | data formatting | bytes 786432 | tf_op jit(solution)/shard_map/all_gather | solution.py:40
  1016.3 0.7 multiply_exponential_fusion
  1017.0 1.6 multiply_add_fusion
  1018.7 2.3 copy.41
  1021.0 7.1 fusion.26
  1028.1 2.5 copy.42
  1030.6 162.1 %all_to_all.36 = f32[6,8,64,128]{3,1,0,2:T(8,128)S(1)} all-to-all(f32[6,8,64,128]{3,1,0,2:T(8,128)S(1)} %copy.42), channel_id=1, replica_groups=mesh['sub'=32,'lev'=16] {'lev'}, dimensions={2} | all-to-all | bytes 3145728 | tf_op jit(solution)/shard_map/all_to_all | solution.py:88
  1192.6 2.6 fusion.37
  1195.3 1.5 fusion.45
  1196.8 0.8 copy.46
  1197.7 41.9 %all_to_all.37 = f32[6,128,4,128]{3,2,0,1:T(4,128)S(1)} all-to-all(f32[6,128,4,128]{3,2,0,1:T(4,128)S(1)} %copy.46), channel_id=1, replica_groups=mesh['sub'=32,'lev'=16] {'lev'}, dimensions={1} | all-to-all | bytes 3145728 | tf_op jit(solution)/shard_map/all_to_all | solution.py:92
  1239.8 1.4 copy.48
  1241.2 2.3 copy.49
  1243.5 9.1 fusion.29
  1252.7 2.8 copy.50
  1255.4 7.2 fusion.42
  1263.1 1225.7 %all-gather.1 = f32[192,8,64,1]{3,1,0,2:T(8,128)} all-gather(f32[6,8,64,1]{3,1,0,2:T(8,128)S(1)} %slice.9), channel_id=3, replica_groups=mesh['sub'=32,'lev'=16] {'sub'}, dimensions={0}, use_global_device_ids=true | all-gather | bytes 405504 | tf_op jit(solution)/shard_map/all_gather | solution.py:40
  2488.8 26.5 %copy.51 = f32[192,8,64,1]{2,1,0,3:T(8,128)S(1)} copy(f32[192,8,64,1]{3,1,0,2:T(8,128)} %all-gather.1) | data formatting | bytes 786432 | tf_op jit(solution)/shard_map/all_gather | solution.py:40
  2516.2 1.6 copy.53
  (49 shorter events, 3.8 us)
Async XLA Ops:
  0.0 1192.6 %copy-start = (f32[6,128,128]{2,1,0:T(8,128)S(1)}, f32[6,128,128]{2,1,0:T(8,128)}, u32[]{:S(2)}) copy-start(f32[6,128,128]{2,1,0:T(8,128)} %param.14) | copy-start | bytes 1179652
  0.1 10.0 copy-start.9
  0.7 9.4 copy-start.7
  2.8 7.3 copy-start.14
  3.6 6.5 copy-start.3
  1192.6 2.7 copy-start.12
  1241.2 2.3 copy-start.2
  1241.2 2.3 copy-start.13
  1252.6 2.8 copy-start.8
  1252.6 2.8 copy-start.10
  1252.6 2.8 copy-start.15
  2488.8 26.6 %copy-start.6 = (f32[32,64]{1,0:T(8,128)S(1)}, f32[32,64]{1,0:T(8,128)}, u32[]{:S(2)}) copy-start(f32[32,64]{1,0:T(8,128)} %get-tuple-element.5) | copy-start | bytes 24580
  2488.8 26.8 %copy-start.4 = (f32[64,128]{1,0:T(8,128)S(1)}, f32[64,128]{1,0:T(8,128)}, u32[]{:S(2)}) copy-start(f32[64,128]{1,0:T(8,128)} %copy-done.3) | copy-start | bytes 98308
  2488.8 26.8 %copy-start.5 = (f32[64,128]{1,0:T(8,128)S(1)}, f32[64,128]{1,0:T(8,128)}, u32[]{:S(2)}) copy-start(f32[64,128]{1,0:T(8,128)} %get-tuple-element.7) | copy-start | bytes 98308
  2488.8 26.9 %copy-start.11 = (f32[6,8]{1,0:T(8,128)S(1)}, f32[6,8]{1,0:T(8,128)}, u32[]{:S(2)}) copy-start(f32[6,8]{1,0:T(8,128)} %param.10) | copy-start | bytes 580
  2515.7 2.1 copy-start.1

commit v2 on v1

v2 whole, which is shorter than its diff:
```python
import functools

import jax
import jax.numpy as jnp
from jax import lax
from jax.experimental import pallas as pl
from jax.experimental.pallas import tpu as pltpu
from jax.sharding import PartitionSpec as P

MESH = pl.DeviceIdType.MESH
HALF = 3
NEAR = 8


def rate_table(length, fast_one, fast_two):
    return jnp.array(
        [
            fast_one,
            fast_two,
            0.3 / length,
            0.6 / length,
            1.0 / length,
            1.4 / length,
            1.8 / length,
            2.2 / length,
        ],
        jnp.float32,
    )


def decay_lookup(classes, rates):
    matches = classes[:, None] == jnp.arange(8, dtype=jnp.int32)[None, :]
    return jnp.sum(jnp.where(matches, jnp.exp(-rates)[None, :], 0.0), axis=1)


def tables_along_x(decays, span, blocks):
    lane = jnp.arange(span)
    log_decay = jnp.log(decays)
    powers, doubling = decays, []
    for k in range(span.bit_length() - 1):
        doubling.append(powers)
        powers = powers * powers
    offsets = 2 ** jnp.arange(len(doubling))
    doubling = jnp.stack(doubling, axis=1)[:, :, None]
    ahead = (lane[None, :] + offsets[:, None] < span)[None]
    behind = (lane[None, :] >= offsets[:, None])[None]
    entering_b = jnp.exp((span - lane).astype(jnp.float32)[None] * log_decay[:, None])
    entering_f = jnp.exp((lane + 1).astype(jnp.float32)[None] * log_decay[:, None])
    steps_b = jnp.concatenate([jnp.where(ahead, doubling, 0.0), entering_b[:, None]], axis=1)
    steps_f = jnp.concatenate([jnp.where(behind, doubling, 0.0), entering_f[:, None]], axis=1)

    me = lax.axis_index("sub")
    mine, block = me % NEAR, me // NEAR
    near, far = jnp.arange(NEAR), jnp.arange(blocks)

    def power(gap):
        reach = jnp.maximum(gap, 0).astype(jnp.float32) * span
        grown = jnp.exp(reach[:, None] * log_decay[None])
        return jnp.where((gap >= 0)[:, None], grown, 0.0)

    def gated(keep, gap):
        return jnp.where(keep[:, None], power(gap), 0.0)

    mix = jnp.concatenate(
        [
            power(near - mine - 1),
            power(near),
            gated(far > block, NEAR * (far - block - 1) + NEAR - 1 - mine),
            power(mine - near - 1),
            power(NEAR - 1 - near),
            gated(far < block, NEAR * (block - far - 1) + mine),
        ]
    )
    return steps_b, steps_f, jnp.pad(mix, ((0, 0), (0, span - mix.shape[1])))


def kernel(
    subs,
    levs,
    field_ref,
    std_ref,
    land_ref,
    gain_ref,
    steps_b_ref,
    steps_f_ref,
    mix_ref,
    cols_ref,
    modes_ref,
    variance_ref,
    out_ref,
    slab,
    gathered,
    mixed,
    returned,
    work,
    packed,
    near_in,
    block_sum,
    far_in,
    matrix,
    in_send,
    in_recv,
    out_send,
    out_recv,
    near_send,
    near_recv,
    far_send,
    far_recv,
):
    sub, lev = lax.axis_index("sub"), lax.axis_index("lev")
    mine, block = sub % NEAR, sub // NEAR
    blocks = subs // NEAR
    rows = land_ref.shape[0]
    span = land_ref.shape[1]
    share = rows // levs
    tall = slab.shape[2]
    doublings = span.bit_length() - 1
    lanes = lax.broadcasted_iota(jnp.int32, (tall, span), 1)

    def lev_peer(k):
        return (lev + k) % levs

    def near_peer(k):
        return block * NEAR + (mine + k) % NEAR

    def far_peer(k):
        return ((block + k) % blocks) * NEAR + mine

    barrier = pltpu.get_barrier_semaphore()

    @pl.loop(1, levs)
    def _(k):
        pl.semaphore_signal(barrier, inc=1, device_id=(sub, lev_peer(k)), device_id_type=MESH)

    @pl.loop(1, NEAR)
    def _(k):
        pl.semaphore_signal(barrier, inc=1, device_id=(near_peer(k), lev), device_id_type=MESH)

    @pl.loop(1, blocks)
    def _(k):
        pl.semaphore_signal(barrier, inc=1, device_id=(far_peer(k), lev), device_id_type=MESH)

    def weight(half, y):
        return std_ref[pl.ds(half * tall, tall), :] * land_ref[pl.ds(y, 1), :]

    def natural(half, y):
        return pl.ds(half * tall * rows + y, tall, stride=rows)

    def load_weighted(half, y):
        return field_ref[natural(half, y), :] * weight(half, y)

    def remote(src, dst, send, recv, target):
        return pltpu.make_async_remote_copy(
            src_ref=src, dst_ref=dst, send_sem=send, recv_sem=recv,
            device_id=target, device_id_type=MESH,
        )

    def whole(ref, sem):
        pltpu.make_async_copy(ref, ref, sem).wait()

    def lanes_of(v):
        return pl.ds(v * 8, 8)

    def send_levels(half, v):
        def part(peer):
            return slab.at[half, pl.ds(peer * share, share), lanes_of(v), :]

        place = gathered.at[half, v, :, pl.ds(lev * 8, 8), :]

        @pl.loop(1, levs)
        def _(k):
            peer = lev_peer(k)
            remote(part(peer), place, in_send.at[half, v], in_recv.at[half, v], (sub, peer)).start()

        pltpu.make_async_copy(part(lev), place, in_recv.at[half, v]).start()

    def send_back(half, v):
        def part(peer):
            return mixed.at[half, v, :, pl.ds(peer * 8, 8), :]

        place = returned.at[half, pl.ds(lev * share, share), lanes_of(v), :]

        @pl.loop(1, levs)
        def _(k):
            peer = lev_peer(k)
            remote(part(peer), place, out_send.at[half, v], out_recv.at[half, v], (sub, peer)).start()

        pltpu.make_async_copy(part(lev), place, out_recv.at[half, v]).start()

    def make_matrix(var):
        modes = modes_ref[var]
        product = lax.dot_general(
            modes * variance_ref[var], modes, (((1,), (1,)), ((), ())),
            precision=lax.Precision.HIGHEST, preferred_element_type=jnp.float32,
        )
        high = product.astype(jnp.bfloat16)
        matrix[var, :, : high.shape[1]] = high
        matrix[var, :, high.shape[1] :] = (product - high.astype(jnp.float32)).astype(jnp.bfloat16)

    def mix_levels(half, v):
        whole(gathered.at[half, v], in_recv.at[half, v])
        both = matrix[half * HALF + v]
        high_part = both[:, : both.shape[1] // 2]
        for r in range(share):
            value = gathered[half, v, r]
            high = value.astype(jnp.bfloat16)
            low = (value - high.astype(jnp.float32)).astype(jnp.bfloat16)
            mixed[half, v, r] = jnp.dot(
                both, jnp.concatenate([high, high], axis=0), preferred_element_type=jnp.float32
            ) + jnp.dot(high_part, low, preferred_element_type=jnp.float32)
        send_back(half, v)

    def doubled(value, steps, y, backward):
        for k in range(doublings):
            shift = span - 2**k if backward else 2**k
            value = value + steps[y, k : k + 1, :] * pltpu.roll(value, shift, 1)
        return value

    def send_near(half, way):
        place = near_in.at[half, way, mine]

        @pl.loop(1, NEAR)
        def _(k):
            remote(
                packed.at[half, way], place, near_send.at[half, way],
                near_recv.at[half, way], (near_peer(k), lev),
            ).start()

        pltpu.make_async_copy(packed.at[half, way], place, near_recv.at[half, way]).start()

    def factor(way, row):
        return mix_ref[pl.ds(way * (2 * NEAR + blocks) + row, 1), :]

    def send_far(half, way):
        whole(near_in.at[half, way], near_recv.at[half, way])
        total = jnp.zeros((tall, span), jnp.float32)
        for j in range(NEAR):
            total = total + factor(way, NEAR + j) * near_in[half, way, j]
        block_sum[half, way] = total
        place = far_in.at[half, way, block]

        @pl.loop(1, blocks)
        def _(k):
            remote(
                block_sum.at[half, way], place, far_send.at[half, way],
                far_recv.at[half, way], (far_peer(k), lev),
            ).start()

        pltpu.make_async_copy(block_sum.at[half, way], place, far_recv.at[half, way]).start()

    def incoming(half, way):
        total = jnp.zeros((tall, span), jnp.float32)
        for j in range(NEAR):
            total = total + factor(way, j) * near_in[half, way, j]
        whole(far_in.at[half, way], far_recv.at[half, way])
        for j in range(blocks):
            total = total + factor(way, 2 * NEAR + j) * far_in[half, way, j]
        return total

    def spread(state, y):
        return jnp.broadcast_to(pltpu.roll(state, (span - y) % span, 1)[:, 0:1], (tall, span))

    together = 4

    def first_sweep(half, load):
        def body(i, pack):
            for u in range(together):
                y = i * together + u
                value = doubled(load(y) * gain_ref[pl.ds(y, 1), :], steps_b_ref, y, True)
                work[half, y] = value
                pack = jnp.where(lanes == y, pltpu.roll(value, y, 1), pack)
            return pack

        packed[half, 0] = lax.fori_loop(
            0, rows // together, body, jnp.zeros((tall, span), jnp.float32)
        )
        send_near(half, 0)

    def second_sweep(half):
        state = incoming(half, 0)
        decay, scaling = cols_ref[0:1, :], cols_ref[1:2, :]

        def down(i, carried):
            for u in range(together):
                y = rows - 1 - (i * together + u)
                entered = work[half, y] + steps_b_ref[y, doublings : doublings + 1, :] * spread(state, y)
                carried = decay * carried + scaling * entered
                work[half, y] = carried
            return carried

        zero = jnp.zeros((tall, span), jnp.float32)
        lax.fori_loop(0, rows // together, down, zero)

        def up(i, both):
            carried, pack = both
            for u in range(together):
                y = i * together + u
                carried = decay * carried + scaling * work[half, y]
                value = doubled(carried * gain_ref[pl.ds(y, 1), :], steps_f_ref, y, False)
                work[half, y] = value
                pack = jnp.where(lanes == y, pltpu.roll(value, y + 1, 1), pack)
            return carried, pack

        packed[half, 1] = lax.fori_loop(0, rows // together, up, (zero, zero))[1]
        send_near(half, 1)

    def last_sweep(half, store):
        state = incoming(half, 1)

        @pl.loop(0, rows // together)
        def _(i):
            for u in range(together):
                y = i * together + u
                store(y, work[half, y] + steps_f_ref[y, doublings : doublings + 1, :] * spread(state, y))

    @pl.loop(0, rows // together)
    def _(i):
        for u in range(together):
            y = i * together + u
            slab[0, y] = load_weighted(0, y)

    pl.semaphore_wait(barrier, levs + NEAR + blocks - 3)

    for v in range(HALF):
        send_levels(0, v)
    first_sweep(1, lambda y: load_weighted(1, y))

    @pl.loop(0, 2 * HALF)
    def _(var):
        make_matrix(var)

    send_far(1, 0)
    mix_levels(0, 0)
    second_sweep(1)
    mix_levels(0, 1)
    send_far(1, 1)
    mix_levels(0, 2)

    def to_slab(y, value):
        slab[1, y] = value

    last_sweep(1, to_slab)
    for v in range(HALF):
        send_levels(1, v)

    for v in range(HALF):
        whole(returned.at[0, :, lanes_of(v), :], out_recv.at[0, v])
    first_sweep(0, lambda y: returned[0, y])
    mix_levels(1, 0)
    send_far(0, 0)
    mix_levels(1, 1)
    second_sweep(0)
    mix_levels(1, 2)
    send_far(0, 1)

    def to_output(y, value):
        out_ref[natural(0, y), :] = value * weight(0, y)

    last_sweep(0, to_output)

    for v in range(HALF):
        whole(returned.at[1, :, lanes_of(v), :], out_recv.at[1, v])

    @pl.loop(0, rows // together)
    def _(i):
        for u in range(together):
            y = i * together + u
            out_ref[natural(1, y), :] = returned[1, y] * weight(1, y)

    for half in range(2):
        for v in range(HALF):
            sent = gathered.at[half, v, :, pl.ds(0, (levs - 1) * 8), :]
            whole(sent, in_send.at[half, v])
            whole(sent, out_send.at[half, v])
        for way in range(2):
            whole(near_in.at[half, way, pl.ds(0, NEAR - 1)], near_send.at[half, way])
            whole(far_in.at[half, way, pl.ds(0, blocks - 1)], far_send.at[half, way])


def on_device(
    increment, std_dev, land_mask, row_class, column_class, vertical_modes, mode_variance
):
    variables, levels, rows, span = increment.shape
    subs, levs = lax.axis_size("sub"), lax.axis_size("lev")
    blocks = subs // NEAR
    decay_rows = decay_lookup(row_class, rate_table(span * subs, 1.0 / 24, 1.0 / 40))
    decay_cols = decay_lookup(column_class, rate_table(rows, 1.0 / 8, 1.0 / 12))
    gain_rows = jnp.sqrt(1.0 - decay_rows * decay_rows)
    gain_cols = jnp.sqrt(1.0 - decay_cols * decay_cols)
    steps_b, steps_f, mix = tables_along_x(decay_rows, span, blocks)
    tall = HALF * levels
    deep = levels * levs
    share = rows // levs
    f32 = jnp.float32
    result = pl.pallas_call(
        functools.partial(kernel, subs, levs),
        out_shape=jax.ShapeDtypeStruct((variables * levels * rows, span), f32),
        in_specs=[pl.BlockSpec(memory_space=pltpu.VMEM)] * 10,
        out_specs=pl.BlockSpec(memory_space=pltpu.VMEM),
        scratch_shapes=[
            pltpu.VMEM((2, rows, tall, span), f32),
            pltpu.VMEM((2, HALF, share, deep, span), f32),
            pltpu.VMEM((2, HALF, share, deep, span), f32),
            pltpu.VMEM((2, rows, tall, span), f32),
            pltpu.VMEM((2, rows, tall, span), f32),
            pltpu.VMEM((2, 2, tall, span), f32),
            pltpu.VMEM((2, 2, NEAR, tall, span), f32),
            pltpu.VMEM((2, 2, tall, span), f32),
            pltpu.VMEM((2, 2, blocks, tall, span), f32),
            pltpu.VMEM((variables, deep, 2 * deep), jnp.bfloat16),
            pltpu.SemaphoreType.DMA((2, HALF)),
            pltpu.SemaphoreType.DMA((2, HALF)),
            pltpu.SemaphoreType.DMA((2, HALF)),
            pltpu.SemaphoreType.DMA((2, HALF)),
            pltpu.SemaphoreType.DMA((2, 2)),
            pltpu.SemaphoreType.DMA((2, 2)),
            pltpu.SemaphoreType.DMA((2, 2)),
            pltpu.SemaphoreType.DMA((2, 2)),
        ],
        compiler_params=pltpu.CompilerParams(
            collective_id=0, has_side_effects=True, vmem_limit_bytes=40 * 2**20
        ),
    )(
        increment.reshape(variables * levels * rows, span),
        jnp.broadcast_to(std_dev.reshape(variables * levels, 1), (variables * levels, span)),
        1.0 + 0.8 * land_mask.astype(f32),
        jnp.broadcast_to(gain_rows[:, None], (rows, span)),
        steps_b,
        steps_f,
        mix,
        jnp.stack([decay_cols, gain_cols]),
        vertical_modes,
        mode_variance[:, None, :],
    )
    return result.reshape(increment.shape)


def solution(mesh):
    return jax.shard_map(
        on_device,
        mesh=mesh,
        in_specs=(
            P(None, "lev", None, "sub"),
            P(None, "lev"),
            P(None, "sub"),
            P(),
            P("sub"),
            P(),
            P(),
        ),
        out_specs=P(None, "lev", None, "sub"),
        check_vma=False,
    )
```

time: 2520 us -> 127 us (0.05)
  the two profiles are of different devices: /device:TPU:75 before, /device:TPU:64 now
where the time goes in v2:
time: 127 us
  Pallas kernels  120 us (94%)
  other arithmetic  3.15 us (2%)
  local copies, waits for them, and re-layouts  3.1 us (2%)
    pallas_call x1, Pallas kernels, on_device(): pl.pallas_call(functools.partial(kernel, subs, levs), out_shape=jax.Shape...  120 us

profile of v2, /device:TPU:64, one launch (start us, length us, event | category | flops | bytes accessed | tf_op | source)
XLA Modules:
  0.0 126.7 jit_solution(4803585945679452445)
XLA Ops:
  0.0 0.0 copy-start.1
  0.0 0.0 copy-start
  0.0 0.9 select_reduce_fusion.1
  0.9 0.8 select_reduce_fusion
  1.7 0.8 broadcast_in_dim.170
  2.5 0.1 select_select_fusion
  2.7 0.1 iota_compare_fusion.1
  2.7 0.7 broadcast_in_dim.190.variance_ref
  3.5 0.1 exponential_select_fusion
  3.5 0.2 concatenate.11
  3.8 0.1 broadcast_in_dim.171.std_ref
  3.8 0.1 copy.12
  3.9 0.1 broadcast_in_dim.174.gain_ref
  4.0 0.1 multiply_exponential_fusion
  4.2 0.8 multiply_add_fusion.land_ref
  4.9 0.1 broadcast_select_fusion
  5.1 0.1 pad_maximum_fusion
  5.2 0.0 copy-done.1
  5.2 0.0 copy-done
  5.2 120.4 %shard_map.91 = f32[3072,128]{1,0:T(8,128)S(1)} custom-call(f32[3072,128]{1,0:T(8,128)S(1)} %bitcast.19, f32[48,128]{1,0:T(8,128)S(1)} %broadcast_in_dim.171.std_ref, f32[64,128]{1,0:T(8,128)S(1)} %multiply_add_fusion.land_ref, f32[64,128]{1,0:T(8,128)S(1)} %broadcast_in_dim.174.gain_ref, f32[64,8,128]{2,1,0:T(8,128)S(1)} %get-tuple-element.25.steps_b_ref, ...), custom_call_target="tpu_custom_call" | custom-call | tf_op jit(solution)/shard_map/pallas_call | solution.py:395
  125.6 1.1 copy.16
  (18 shorter events, 0.2 us)
Async XLA Ops:
  0.0 5.2 %copy-start.1 = (f32[6,128,128]{2,1,0:T(8,128)S(1)}, f32[6,128,128]{2,1,0:T(8,128)}, u32[]{:S(2)}) copy-start(f32[6,128,128]{2,1,0:T(8,128)} %modes_ref.1) | copy-start | bytes 1179652
  0.0 5.2 %copy-start = (f32[6,8,64,128]{3,2,1,0:T(8,128)S(1)}, f32[6,8,64,128]{3,2,1,0:T(8,128)}, u32[]{:S(2)}) copy-start(f32[6,8,64,128]{3,2,1,0:T(8,128)} %param.9) | copy-start | bytes 4718596

commit v3 on v2

--- a/solution.py
+++ b/solution.py
@@ -113,12 +113,21 @@
     rows = land_ref.shape[0]
     span = land_ref.shape[1]
     share = rows // levs
-    tall = slab.shape[2]
+    tall = work.shape[2]
+    deep = matrix.shape[1]
     doublings = span.bit_length() - 1
     lanes = lax.broadcasted_iota(jnp.int32, (tall, span), 1)
 
+    wide = levs // 4
+
     def lev_peer(k):
-        return (lev + k) % levs
+        order = (k - 1) // 2
+        far = 4 * (order // 2) + 2 + order % 2
+        close = 4 * ((order + 1) // 2) + (order + 1) % 2
+        other = far + (close - far) * ((k - 1) % 2)
+        low = (lev % 2 + other % 2) % 2
+        high = (lev // 2 % 2 + other // 2 % 2) % 2
+        return (lev // 4 + other // 4) % wide * 4 + high * 2 + low
 
     def near_peer(k):
         return block * NEAR + (mine + k) % NEAR
@@ -141,7 +150,7 @@
         pl.semaphore_signal(barrier, inc=1, device_id=(far_peer(k), lev), device_id_type=MESH)
 
     def weight(half, y):
-        return std_ref[pl.ds(half * tall, tall), :] * land_ref[pl.ds(y, 1), :]
+        return std_ref[pl.ds(half * tall, tall), :] * (1.0 + 0.8 * land_ref[pl.ds(y, 1), :].astype(jnp.float32))
 
     def natural(half, y):
         return pl.ds(half * tall * rows + y, tall, stride=rows)
@@ -158,14 +167,14 @@
     def whole(ref, sem):
         pltpu.make_async_copy(ref, ref, sem).wait()
 
-    def lanes_of(v):
-        return pl.ds(v * 8, 8)
+    def read(ref, half, y):
+        return jnp.concatenate([ref[half, v, y] for v in range(HALF)], axis=0)
 
     def send_levels(half, v):
         def part(peer):
-            return slab.at[half, pl.ds(peer * share, share), lanes_of(v), :]
-
-        place = gathered.at[half, v, :, pl.ds(lev * 8, 8), :]
+            return slab.at[half, v, pl.ds(peer * share, share)]
+
+        place = gathered.at[half, v, lev]
 
         @pl.loop(1, levs)
         def _(k):
@@ -176,9 +185,9 @@
 
     def send_back(half, v):
         def part(peer):
-            return mixed.at[half, v, :, pl.ds(peer * 8, 8), :]
-
-        place = returned.at[half, pl.ds(lev * share, share), lanes_of(v), :]
+            return mixed.at[half, v, peer]
+
+        place = returned.at[half, v, pl.ds(lev * share, share)]
 
         @pl.loop(1, levs)
         def _(k):
@@ -190,7 +199,7 @@
     def make_matrix(var):
         modes = modes_ref[var]
         product = lax.dot_general(
-            modes * variance_ref[var], modes, (((1,), (1,)), ((), ())),
+            modes * variance_ref[pl.ds(var, 1), :], modes, (((1,), (1,)), ((), ())),
             precision=lax.Precision.HIGHEST, preferred_element_type=jnp.float32,
         )
         high = product.astype(jnp.bfloat16)
@@ -202,12 +211,13 @@
         both = matrix[half * HALF + v]
         high_part = both[:, : both.shape[1] // 2]
         for r in range(share):
-            value = gathered[half, v, r]
+            value = gathered[half, v, :, r].reshape(deep, span)
             high = value.astype(jnp.bfloat16)
             low = (value - high.astype(jnp.float32)).astype(jnp.bfloat16)
-            mixed[half, v, r] = jnp.dot(
+            product = jnp.dot(
                 both, jnp.concatenate([high, high], axis=0), preferred_element_type=jnp.float32
             ) + jnp.dot(high_part, low, preferred_element_type=jnp.float32)
+            mixed[half, v, :, r] = product.reshape(levs, deep // levs, span)
         send_back(half, v)
 
     def doubled(value, steps, y, backward):
@@ -260,7 +270,11 @@
     def spread(state, y):
         return jnp.broadcast_to(pltpu.roll(state, (span - y) % span, 1)[:, 0:1], (tall, span))
 
-    together = 4
+    def to_slab(half, y, value):
+        for v in range(HALF):
+            slab[half, v, y] = value[v * 8 : v * 8 + 8]
+
+    together = 16
 
     def first_sweep(half, load):
         def body(i, pack):
@@ -317,7 +331,7 @@
     def _(i):
         for u in range(together):
             y = i * together + u
-            slab[0, y] = load_weighted(0, y)
+            to_slab(0, y, load_weighted(0, y))
 
     pl.semaphore_wait(barrier, levs + NEAR + blocks - 3)
 
@@ -336,16 +350,13 @@
     send_far(1, 1)
     mix_levels(0, 2)
 
-    def to_slab(y, value):
-        slab[1, y] = value
-
-    last_sweep(1, to_slab)
+    last_sweep(1, lambda y, value: to_slab(1, y, value))
     for v in range(HALF):
         send_levels(1, v)
 
     for v in range(HALF):
-        whole(returned.at[0, :, lanes_of(v), :], out_recv.at[0, v])
-    first_sweep(0, lambda y: returned[0, y])
+        whole(returned.at[0, v], out_recv.at[0, v])
+    first_sweep(0, lambda y: read(returned, 0, y))
     mix_levels(1, 0)
     send_far(0, 0)
     mix_levels(1, 1)
@@ -359,17 +370,17 @@
     last_sweep(0, to_output)
 
     for v in range(HALF):
-        whole(returned.at[1, :, lanes_of(v), :], out_recv.at[1, v])
+        whole(returned.at[1, v], out_recv.at[1, v])
 
     @pl.loop(0, rows // together)
     def _(i):
         for u in range(together):
             y = i * together + u
-            out_ref[natural(1, y), :] = returned[1, y] * weight(1, y)
+            out_ref[natural(1, y), :] = read(returned, 1, y) * weight(1, y)
 
     for half in range(2):
         for v in range(HALF):
-            sent = gathered.at[half, v, :, pl.ds(0, (levs - 1) * 8), :]
+            sent = gathered.at[half, v, pl.ds(0, levs - 1)]
             whole(sent, in_send.at[half, v])
             whole(sent, out_send.at[half, v])
         for way in range(2):
@@ -398,10 +409,10 @@
         in_specs=[pl.BlockSpec(memory_space=pltpu.VMEM)] * 10,
         out_specs=pl.BlockSpec(memory_space=pltpu.VMEM),
         scratch_shapes=[
-            pltpu.VMEM((2, rows, tall, span), f32),
-            pltpu.VMEM((2, HALF, share, deep, span), f32),
-            pltpu.VMEM((2, HALF, share, deep, span), f32),
-            pltpu.VMEM((2, rows, tall, span), f32),
+            pltpu.VMEM((2, HALF, rows, levels, span), f32),
+            pltpu.VMEM((2, HALF, levs, share, levels, span), f32),
+            pltpu.VMEM((2, HALF, levs, share, levels, span), f32),
+            pltpu.VMEM((2, HALF, rows, levels, span), f32),
             pltpu.VMEM((2, rows, tall, span), f32),
             pltpu.VMEM((2, 2, tall, span), f32),
             pltpu.VMEM((2, 2, NEAR, tall, span), f32),
@@ -423,14 +434,14 @@
     )(
         increment.reshape(variables * levels * rows, span),
         jnp.broadcast_to(std_dev.reshape(variables * levels, 1), (variables * levels, span)),
-        1.0 + 0.8 * land_mask.astype(f32),
+        land_mask,
         jnp.broadcast_to(gain_rows[:, None], (rows, span)),
         steps_b,
         steps_f,
         mix,
         jnp.stack([decay_cols, gain_cols]),
         vertical_modes,
-        mode_variance[:, None, :],
+        mode_variance,
     )
     return result.reshape(increment.shape)
 

time: 127 us -> 110 us (0.87)
  the two profiles are of different devices: /device:TPU:64 before, /device:TPU:48 now
where the time goes in v3:
time: 110 us
  Pallas kernels  105 us (95%)
  local copies, waits for them, and re-layouts  2.42 us (2%)
  other arithmetic  2.38 us (2%)
    pallas_call x1, Pallas kernels, on_device(): pl.pallas_call(functools.partial(kernel, subs, levs), out_shape=jax.Shape...  105 us

profile of v3, /device:TPU:48, one launch (start us, length us, event | category | flops | bytes accessed | tf_op | source)
XLA Modules:
  0.0 109.5 jit_solution(14335342511536829825)
XLA Ops:
  0.0 0.0 copy-start.3
  0.0 0.0 copy-start.1
  0.0 0.0 copy-start.2
  0.0 0.0 copy-start
  0.0 0.9 select_reduce_fusion.1
  0.9 0.8 select_reduce_fusion
  1.7 0.8 broadcast_in_dim.167
  2.6 0.1 select_select_fusion
  2.7 0.1 iota_compare_fusion.1
  2.8 0.1 exponential_select_fusion
  2.9 0.2 concatenate.11
  3.1 0.1 broadcast_in_dim.168.std_ref
  3.2 0.1 copy.12
  3.3 0.1 broadcast_in_dim.171.gain_ref
  3.4 0.1 multiply_exponential_fusion
  3.5 0.1 broadcast_select_fusion
  3.7 0.1 pad_maximum_fusion
  3.8 0.0 copy-done.3
  3.8 0.0 copy-done.1
  3.8 0.0 copy-done.2
  3.8 0.0 copy-done
  3.8 104.6 %shard_map.91 = f32[3072,128]{1,0:T(8,128)S(1)} custom-call(f32[3072,128]{1,0:T(8,128)S(1)} %bitcast.19, f32[48,128]{1,0:T(8,128)S(1)} %broadcast_in_dim.168.std_ref, s32[64,128]{1,0:T(8,128)S(1)} %copy-done.2, f32[64,128]{1,0:T(8,128)S(1)} %broadcast_in_dim.171.gain_ref, f32[64,8,128]{2,1,0:T(8,128)S(1)} %get-tuple-element.25.steps_b_ref, ...), custom_call_target="tpu_custom_call" | custom-call | tf_op jit(solution)/shard_map/pallas_call | solution.py:406
  108.4 1.1 %copy.16 = f32[6,8,64,128]{3,2,1,0:T(8,128)} copy(f32[6,8,64,128]{3,2,1,0:T(8,128)S(1)} %bitcast.18) | data formatting | bytes 3145728
  (18 shorter events, 0.2 us)
Async XLA Ops:
  0.0 3.8 %copy-start.3 = (f32[6,128]{1,0:T(8,128)S(1)}, f32[6,128]{1,0:T(8,128)}, u32[]{:S(2)}) copy-start(f32[6,128]{1,0:T(8,128)} %variance_ref.1) | copy-start | bytes 9220
  0.0 3.8 %copy-start.1 = (f32[6,128,128]{2,1,0:T(8,128)S(1)}, f32[6,128,128]{2,1,0:T(8,128)}, u32[]{:S(2)}) copy-start(f32[6,128,128]{2,1,0:T(8,128)} %modes_ref.1) | copy-start | bytes 1179652
  0.0 3.8 %copy-start.2 = (s32[64,128]{1,0:T(8,128)S(1)}, s32[64,128]{1,0:T(8,128)}, u32[]{:S(2)}) copy-start(s32[64,128]{1,0:T(8,128)} %land_ref.1) | copy-start | bytes 98308
  0.0 3.8 %copy-start = (f32[6,8,64,128]{3,2,1,0:T(8,128)S(1)}, f32[6,8,64,128]{3,2,1,0:T(8,128)}, u32[]{:S(2)}) copy-start(f32[6,8,64,128]{3,2,1,0:T(8,128)} %param.9) | copy-start | bytes 4718596

commit v4 on v3

--- a/solution.py
+++ b/solution.py
@@ -78,7 +78,7 @@
     subs,
     levs,
     field_ref,
-    std_ref,
+    deviation_ref,
     land_ref,
     gain_ref,
     steps_b_ref,
@@ -98,6 +98,7 @@
     block_sum,
     far_in,
     matrix,
+    std_ref,
     in_send,
     in_recv,
     out_send,
@@ -149,6 +150,15 @@
     def _(k):
         pl.semaphore_signal(barrier, inc=1, device_id=(far_peer(k), lev), device_id_type=MESH)
 
+    eight = deviation_ref.shape[1]
+    diagonal = lax.broadcasted_iota(jnp.int32, (eight, eight), 0) == lax.broadcasted_iota(
+        jnp.int32, (eight, eight), 1
+    )
+    for v in range(2 * HALF):
+        across = jnp.broadcast_to(deviation_ref[v : v + 1, :], (eight, eight))
+        upright = jnp.sum(jnp.where(diagonal, across, 0.0), axis=1, keepdims=True)
+        std_ref[v * eight : (v + 1) * eight, :] = jnp.broadcast_to(upright, (eight, span))
+
     def weight(half, y):
         return std_ref[pl.ds(half * tall, tall), :] * (1.0 + 0.8 * land_ref[pl.ds(y, 1), :].astype(jnp.float32))
 
@@ -288,7 +298,6 @@
         packed[half, 0] = lax.fori_loop(
             0, rows // together, body, jnp.zeros((tall, span), jnp.float32)
         )
-        send_near(half, 0)
 
     def second_sweep(half):
         state = incoming(half, 0)
@@ -333,36 +342,39 @@
             y = i * together + u
             to_slab(0, y, load_weighted(0, y))
 
+    first_sweep(1, lambda y: load_weighted(1, y))
     pl.semaphore_wait(barrier, levs + NEAR + blocks - 3)
 
-    for v in range(HALF):
-        send_levels(0, v)
-    first_sweep(1, lambda y: load_weighted(1, y))
+    send_near(1, 0)
+    send_levels(0, 0)
+    send_far(1, 0)
+    send_levels(0, 1)
+    send_levels(0, 2)
 
     @pl.loop(0, 2 * HALF)
     def _(var):
         make_matrix(var)
 
-    send_far(1, 0)
     mix_levels(0, 0)
     second_sweep(1)
+    send_far(1, 1)
     mix_levels(0, 1)
-    send_far(1, 1)
     mix_levels(0, 2)
-
     last_sweep(1, lambda y, value: to_slab(1, y, value))
-    for v in range(HALF):
-        send_levels(1, v)
-
+
+    send_levels(1, 0)
     for v in range(HALF):
         whole(returned.at[0, v], out_recv.at[0, v])
     first_sweep(0, lambda y: read(returned, 0, y))
+    send_near(0, 0)
+    send_far(0, 0)
+    send_levels(1, 1)
+    send_levels(1, 2)
     mix_levels(1, 0)
-    send_far(0, 0)
+    second_sweep(0)
+    send_far(0, 1)
     mix_levels(1, 1)
-    second_sweep(0)
     mix_levels(1, 2)
-    send_far(0, 1)
 
     def to_output(y, value):
         out_ref[natural(0, y), :] = value * weight(0, y)
@@ -419,6 +431,7 @@
             pltpu.VMEM((2, 2, tall, span), f32),
             pltpu.VMEM((2, 2, blocks, tall, span), f32),
             pltpu.VMEM((variables, deep, 2 * deep), jnp.bfloat16),
+            pltpu.VMEM((variables * levels, span), f32),
             pltpu.SemaphoreType.DMA((2, HALF)),
             pltpu.SemaphoreType.DMA((2, HALF)),
             pltpu.SemaphoreType.DMA((2, HALF)),
@@ -433,7 +446,7 @@
         ),
     )(
         increment.reshape(variables * levels * rows, span),
-        jnp.broadcast_to(std_dev.reshape(variables * levels, 1), (variables * levels, span)),
+        std_dev,
         land_mask,
         jnp.broadcast_to(gain_rows[:, None], (rows, span)),
         steps_b,

time: 110 us -> 109 us (level)
  the two profiles are of different devices: /device:TPU:48 before, /device:TPU:1 now
where the time goes in v4:
time: 109 us; the launch traced here: 108 us
  Pallas kernels  104 us (95%)
  other arithmetic  2.38 us (2%)
  local copies, waits for them, and re-layouts  1.58 us (1%)
    pallas_call x1, Pallas kernels, on_device(): pl.pallas_call(functools.partial(kernel, subs, levs), out_shape=jax.Shape...  104 us

profile of v4, /device:TPU:1, one launch (start us, length us, event | category | flops | bytes accessed | tf_op | source)
XLA Modules:
  0.0 108.4 jit_solution(6268321935613566402)
XLA Ops:
  0.0 0.0 copy-start.4
  0.0 0.0 copy-start.1
  0.0 0.0 copy-start.2
  0.0 0.0 copy-start.3
  0.0 0.0 copy-start
  0.1 0.9 select_reduce_fusion.1
  0.9 0.8 select_reduce_fusion
  1.8 0.1 select_select_fusion
  2.0 0.1 iota_compare_fusion.1
  2.1 0.1 exponential_select_fusion
  2.1 0.2 concatenate.11
  2.4 0.1 copy.12
  2.5 0.1 broadcast_in_dim.162.gain_ref
  2.5 0.1 multiply_exponential_fusion
  2.7 0.1 broadcast_select_fusion
  2.8 0.1 pad_maximum_fusion
  3.0 0.0 copy-done.4
  3.0 0.0 copy-done.1
  3.0 0.0 copy-done.2
  3.0 0.0 copy-done.3
  3.0 0.0 copy-done
  3.0 104.3 %shard_map.91 = f32[3072,128]{1,0:T(8,128)S(1)} custom-call(f32[3072,128]{1,0:T(8,128)S(1)} %bitcast.19, f32[6,8]{1,0:T(8,128)S(1)} %copy-done.3, s32[64,128]{1,0:T(8,128)S(1)} %copy-done.2, f32[64,128]{1,0:T(8,128)S(1)} %broadcast_in_dim.162.gain_ref, f32[64,8,128]{2,1,0:T(8,128)S(1)} %get-tuple-element.25.steps_b_ref, ...), custom_call_target="tpu_custom_call" | custom-call | tf_op jit(solution)/shard_map/pallas_call | solution.py:418
  107.3 1.1 %copy.16 = f32[6,8,64,128]{3,2,1,0:T(8,128)} copy(f32[6,8,64,128]{3,2,1,0:T(8,128)S(1)} %bitcast.18) | data formatting | bytes 3145728
  (18 shorter events, 0.2 us)
Async XLA Ops:
  0.0 3.0 %copy-start.4 = (f32[6,128]{1,0:T(8,128)S(1)}, f32[6,128]{1,0:T(8,128)}, u32[]{:S(2)}) copy-start(f32[6,128]{1,0:T(8,128)} %variance_ref.1) | copy-start | bytes 9220
  0.0 3.0 %copy-start.1 = (f32[6,128,128]{2,1,0:T(8,128)S(1)}, f32[6,128,128]{2,1,0:T(8,128)}, u32[]{:S(2)}) copy-start(f32[6,128,128]{2,1,0:T(8,128)} %modes_ref.1) | copy-start | bytes 1179652
  0.0 3.0 %copy-start.2 = (s32[64,128]{1,0:T(8,128)S(1)}, s32[64,128]{1,0:T(8,128)}, u32[]{:S(2)}) copy-start(s32[64,128]{1,0:T(8,128)} %land_ref.1) | copy-start | bytes 98308
  0.0 3.0 %copy-start.3 = (f32[6,8]{1,0:T(8,128)S(1)}, f32[6,8]{1,0:T(8,128)}, u32[]{:S(2)}) copy-start(f32[6,8]{1,0:T(8,128)} %deviation_ref.1) | copy-start | bytes 580
  0.0 3.0 %copy-start = (f32[6,8,64,128]{3,2,1,0:T(8,128)S(1)}, f32[6,8,64,128]{3,2,1,0:T(8,128)}, u32[]{:S(2)}) copy-start(f32[6,8,64,128]{3,2,1,0:T(8,128)} %param.9) | copy-start | bytes 4718596

commit v5 on v4

--- a/solution.py
+++ b/solution.py
@@ -256,7 +256,8 @@
         total = jnp.zeros((tall, span), jnp.float32)
         for j in range(NEAR):
             total = total + factor(way, NEAR + j) * near_in[half, way, j]
-        block_sum[half, way] = total
+        block_sum[half, way, 0:8] = total[0:8] + pltpu.roll(total[8:16], span // 2, 1)
+        block_sum[half, way, 8:16] = total[16:24]
         place = far_in.at[half, way, block]
 
         @pl.loop(1, blocks)
@@ -274,7 +275,11 @@
             total = total + factor(way, j) * near_in[half, way, j]
         whole(far_in.at[half, way], far_recv.at[half, way])
         for j in range(blocks):
-            total = total + factor(way, 2 * NEAR + j) * far_in[half, way, j]
+            shared = far_in[half, way, j, 0:8]
+            state = jnp.concatenate(
+                [shared, pltpu.roll(shared, span // 2, 1), far_in[half, way, j, 8:16]], axis=0
+            )
+            total = total + factor(way, 2 * NEAR + j) * state
         return total
 
     def spread(state, y):
@@ -428,8 +433,8 @@
             pltpu.VMEM((2, rows, tall, span), f32),
             pltpu.VMEM((2, 2, tall, span), f32),
             pltpu.VMEM((2, 2, NEAR, tall, span), f32),
-            pltpu.VMEM((2, 2, tall, span), f32),
-            pltpu.VMEM((2, 2, blocks, tall, span), f32),
+            pltpu.VMEM((2, 2, 2 * levels, span), f32),
+            pltpu.VMEM((2, 2, blocks, 2 * levels, span), f32),
             pltpu.VMEM((variables, deep, 2 * deep), jnp.bfloat16),
             pltpu.VMEM((variables * levels, span), f32),
             pltpu.SemaphoreType.DMA((2, HALF)),

time: 109 us -> 106 us (0.972)
  Pallas kernels: 104 us -> 101 us
    pallas_call x1, Pallas kernels: 104 us -> 101 us  [on_device(): pl.pallas_call(functools.partial(kernel, subs, levs), out_shape=jax.Shape...]
where the time goes in v5:
time: 106 us
  Pallas kernels  101 us (95%)
  other arithmetic  2.38 us (2%)
  local copies, waits for them, and re-layouts  1.58 us (1%)
    pallas_call x1, Pallas kernels, on_device(): pl.pallas_call(functools.partial(kernel, subs, levs), out_shape=jax.Shape...  101 us

profile of v5, /device:TPU:1, one launch (start us, length us, event | category | flops | bytes accessed | tf_op | source)
XLA Modules:
  0.0 105.6 jit_solution(390409179780778073)
XLA Ops:
  0.0 0.0 copy-start.4
  0.0 0.0 copy-start.1
  0.0 0.0 copy-start.2
  0.0 0.0 copy-start.3
  0.0 0.0 copy-start
  0.1 0.9 select_reduce_fusion.1
  0.9 0.8 select_reduce_fusion
  1.8 0.1 select_select_fusion
  2.0 0.1 iota_compare_fusion.1
  2.1 0.1 exponential_select_fusion
  2.1 0.2 concatenate.11
  2.4 0.1 copy.12
  2.5 0.1 broadcast_in_dim.162.gain_ref
  2.5 0.1 multiply_exponential_fusion
  2.7 0.1 broadcast_select_fusion
  2.8 0.1 pad_maximum_fusion
  3.0 0.0 copy-done.4
  3.0 0.0 copy-done.1
  3.0 0.0 copy-done.2
  3.0 0.0 copy-done.3
  3.0 0.0 copy-done
  3.0 101.5 %shard_map.91 = f32[3072,128]{1,0:T(8,128)S(1)} custom-call(f32[3072,128]{1,0:T(8,128)S(1)} %bitcast.19, f32[6,8]{1,0:T(8,128)S(1)} %copy-done.3, s32[64,128]{1,0:T(8,128)S(1)} %copy-done.2, f32[64,128]{1,0:T(8,128)S(1)} %broadcast_in_dim.162.gain_ref, f32[64,8,128]{2,1,0:T(8,128)S(1)} %get-tuple-element.25.steps_b_ref, ...), custom_call_target="tpu_custom_call" | custom-call | tf_op jit(solution)/shard_map/pallas_call | solution.py:423
  104.5 1.1 %copy.16 = f32[6,8,64,128]{3,2,1,0:T(8,128)} copy(f32[6,8,64,128]{3,2,1,0:T(8,128)S(1)} %bitcast.18) | data formatting | bytes 3145728
  (18 shorter events, 0.2 us)
Async XLA Ops:
  0.0 3.0 %copy-start.4 = (f32[6,128]{1,0:T(8,128)S(1)}, f32[6,128]{1,0:T(8,128)}, u32[]{:S(2)}) copy-start(f32[6,128]{1,0:T(8,128)} %variance_ref.1) | copy-start | bytes 9220
  0.0 3.0 %copy-start.1 = (f32[6,128,128]{2,1,0:T(8,128)S(1)}, f32[6,128,128]{2,1,0:T(8,128)}, u32[]{:S(2)}) copy-start(f32[6,128,128]{2,1,0:T(8,128)} %modes_ref.1) | copy-start | bytes 1179652
  0.0 3.0 %copy-start.2 = (s32[64,128]{1,0:T(8,128)S(1)}, s32[64,128]{1,0:T(8,128)}, u32[]{:S(2)}) copy-start(s32[64,128]{1,0:T(8,128)} %land_ref.1) | copy-start | bytes 98308
  0.0 3.0 %copy-start.3 = (f32[6,8]{1,0:T(8,128)S(1)}, f32[6,8]{1,0:T(8,128)}, u32[]{:S(2)}) copy-start(f32[6,8]{1,0:T(8,128)} %deviation_ref.1) | copy-start | bytes 580
  0.0 3.0 %copy-start = (f32[6,8,64,128]{3,2,1,0:T(8,128)S(1)}, f32[6,8,64,128]{3,2,1,0:T(8,128)}, u32[]{:S(2)}) copy-start(f32[6,8,64,128]{3,2,1,0:T(8,128)} %param.9) | copy-start | bytes 4718596
